TPU v7x, 256 devices: a whole 4x4x8 slice. The times are simulated.
256 devices in a mesh: row: 32 (over z, x), col: 2 (over core), rep: 4 (over y).
Axes of the slice: x: 4, y: 4, z: 8, core: 2. Of those that a mesh axis runs over, the one named last changes fastest.
Arguments:
- pre_act: bfloat16 [16384, 12288], P(('rep', 'col'), 'row'), may hold values from -8 to 8
- w_out: bfloat16 [12288, 6144], P('row', 'col'), may hold values from -0.0546875 to 0.0546875
- grad_out: bfloat16 [16384, 6144], P(('rep', 'row'), 'col'), may hold values from -6 to 6
Outputs:
- grad_pre: bfloat16 [16384, 12288], P(('rep', 'col'), 'row')
- grad_weight: float32 [12288, 6144], P(('row', 'rep'), 'col')
All inputs are finite; a program needn't handle non-finite values.
Results may differ from a plain program's by a relative error of at most 0.0027.
Values may be sent and summed in bfloat16 or wider, within the bound.
A program may use at most 128 MiB of HBM per device.

v0:
```python
import jax
import jax.numpy as jnp
from jax import lax
from jax.sharding import PartitionSpec as P

SQRT_TWO_PI = 0.7978845608028654
CUBIC = 0.044715


def in_blocks(value, dim, length):
    before, after = (value.shape[:dim], value.shape[dim + 1 :])
    return jnp.moveaxis(value.reshape(*before, length, -1, *after), dim, 0)


def summed_on_arrival(value, axis, dim):
    blocks = in_blocks(value, dim, lax.axis_size(axis))
    arrived = lax.all_to_all(blocks, axis, split_axis=0, concat_axis=0, tiled=True)
    return arrived.sum(axis=0)


def gelu_pair(values):
    inner = SQRT_TWO_PI * (values + CUBIC * values * values * values)
    bent = jnp.tanh(inner)
    output = 0.5 * values * (1.0 + bent)
    slopes = 0.5 * (1.0 + bent) + 0.5 * values * (1.0 - bent * bent) * SQRT_TWO_PI * (
        1.0 + 3.0 * CUBIC * values * values
    )
    return (output, slopes)


def contract_rows(left, right):
    return lax.dot_general(
        left, right, (((0,), (0,)), ((), ())), preferred_element_type=jnp.float32
    )


def on_device(pre_act, w_out, grad_out):
    total_tokens = grad_out.shape[0] * lax.axis_size("row") * lax.axis_size("rep")
    factor = float(total_tokens) ** (-0.5)
    grad_all = lax.all_gather(grad_out, "row", axis=0, tiled=True)
    output, slopes = gelu_pair(pre_act.astype(jnp.float32))
    activation = output.astype(jnp.bfloat16)
    block = grad_all
    grad_act = summed_on_arrival(
        lax.dot_general(block, w_out, (((1,), (1,)), ((), ())), preferred_element_type=jnp.float32),
        "col",
        0,
    )
    grad_pre = (grad_act * slopes).astype(jnp.bfloat16)
    block = grad_all
    whole = contract_rows(lax.all_gather(activation, "col", axis=0, tiled=True), block)
    grad_weight = lax.psum_scatter(whole * factor, "rep", scatter_dimension=0, tiled=True)
    return (grad_pre, grad_weight)


def solution(mesh):
    in_specs = (P(("rep", "col"), "row"), P("row", "col"), P(("rep", "row"), "col"))
    out_specs = (P(("rep", "col"), "row"), P(("row", "rep"), "col"))
    return jax.shard_map(
        on_device, mesh=mesh, in_specs=in_specs, out_specs=out_specs, check_vma=False
    )
```

profile of v0, /device:TPU:1, one launch (start us, length us, event | category | flops | bytes accessed | tf_op | source)
XLA Modules:
  0.0 328.2 jit_solution(14980540281799287659)
XLA Ops:
  7.2 0.0 copy-start
  7.2 0.0 all-gather.3.cloned.1.call-start
  7.2 0.7 all-gather.3.cloned.1.call-update
  7.9 0.0 all-gather.5.cloned.1.call-start
  8.0 189.1 %all-gather.3.cloned.1.call-done = bf16[4096,3072]{1,0:T(8,128)(2,1)} async-done(((bf16[128,3072]{1,0:T(8,128)(2,1)}), bf16[4096,3072]{1,0:T(8,128)(2,1)}) %all-gather.3.cloned.1.call-update) | async-done | bytes 25165840 | tf_op jit(solution)/shard_map/all_gather | solution.py:40
  197.1 0.0 copy-done
  197.1 16.5 %fusion.11 = f32[4096,384]{1,0:T(8,128)S(1)} fusion(bf16[4096,3072]{1,0:T(8,128)(2,1)} %all-gather.3.cloned.1.call-done, bf16[384,3072]{1,0:T(8,128)(2,1)S(1)} %copy-done), kind=kOutput, calls=%fused_computation.19 | convolution fusion | flops 9663676416 | bytes 33816576 | tf_op jit(solution)/shard_map/dot_general | solution.py:45
  213.6 11.1 %all_to_all.5 = f32[2,2048,384]{2,1,0:T(8,128)} all-to-all(f32[2,2048,384]{2,1,0:T(8,128)S(1)} %bitcast.5), channel_id=1, replica_groups=mesh['row'=32,'col'=2,'rep'=4] {'col'}, dimensions={0} | all-to-all | bytes 12582912 | tf_op jit(solution)/shard_map/all_to_all | solution.py:17
  224.7 5.1 %reduce_sum.9 = f32[2048,384]{1,0:T(8,128)} reduce(f32[2,2048,384]{2,1,0:T(8,128)} %all_to_all.5, f32[]{:T(128)} %constant.0.clone.1), dimensions={0}, to_apply=%region_0.0 | reduce | flops 786432 | bytes 9437188 | tf_op jit(solution)/shard_map/reduce_sum | solution.py:18
  229.9 5.1 %fusion.7 = (bf16[2048,384]{1,0:T(8,128)(2,1)}, bf16[2048,384]{1,0:T(8,128)(2,1)}) fusion(bf16[2048,384]{1,0:T(8,128)(2,1)} %param.3, f32[2048,384]{1,0:T(8,128)} %reduce_sum.9), kind=kLoop, calls=%fused_computation.15 | loop fusion | flops 17301504 | bytes 7864320 | tf_op jit(solution)/shard_map/convert_element_type | solution.py:42
  235.0 0.0 all-gather.5.cloned.1.call-update
  235.0 0.0 reduce-scatter.2.cloned.1.call-start
  235.1 15.1 %all-gather.5.cloned.1.call-done = bf16[4096,384]{1,0:T(8,128)(2,1)} async-done(((bf16[2048,384]{1,0:T(8,128)(2,1)}), bf16[4096,384]{1,0:T(8,128)(2,1)}) %all-gather.5.cloned.1.call-update) | async-done | bytes 3145744 | tf_op jit(solution)/shard_map/all_gather | solution.py:51
  250.1 17.1 %convolution_multiply_fusion = f32[384,3072]{1,0:T(8,128)} fusion(bf16[4096,384]{1,0:T(8,128)(2,1)} %all-gather.5.cloned.1.call-done, bf16[4096,3072]{1,0:T(8,128)(2,1)} %all-gather.3.cloned.1.call-done), kind=kOutput, calls=%fused_computation.7 | convolution fusion | flops 9664856064 | bytes 33030144 | tf_op jit(solution)/shard_map/dot_general | solution.py:32
  267.3 0.0 reduce-scatter.2.cloned.1.call-update
  267.3 54.4 %reduce-scatter.2.cloned.1.call-done = f32[96,3072]{1,0:T(8,128)} async-done(((f32[384,3072]{1,0:T(8,128)}), f32[96,3072]{1,0:T(8,128)}) %reduce-scatter.2.cloned.1.call-update) | async-done | bytes 1179664 | tf_op jit(solution)/shard_map/reduce_scatter | solution.py:52
Async XLA Ops:
  7.2 189.9 %copy-start = (bf16[384,3072]{1,0:T(8,128)(2,1)S(1)}, bf16[384,3072]{1,0:T(8,128)(2,1)}, u32[]{:S(2)}) copy-start(bf16[384,3072]{1,0:T(8,128)(2,1)} %param.4) | copy-start | bytes 7077892
  7.2 189.9 %all-gather.3.cloned.1.call-start = ((), (), s32[]{:S(2)}) async-start(), calls=%async_computation.2 | async-start | bytes 25952256 | tf_op jit(solution)/shard_map/all_gather | solution.py:40
  7.9 242.2 %all-gather.5.cloned.1.call-start = ((), (), s32[]{:S(2)}) async-start(), calls=%async_computation.3 | async-start | bytes 4718592 | tf_op jit(solution)/shard_map/all_gather | solution.py:51
  235.0 86.6 %reduce-scatter.2.cloned.1.call-start = ((), (), s32[]{:S(2)}) async-start(), calls=%async_computation.4 | async-start | bytes 5898240 | tf_op jit(solution)/shard_map/reduce_scatter | solution.py:52
Sparse Core Ops, SparseCore 0:
  10.6 186.4 all-gather.2
  235.1 14.9 all-gather.4
  267.4 54.1 reduce-scatter.1
where the time goes:
time: 328 us
  waiting for transfers between devices  259 us (79%)
  matrix products  33.6 us (10%)
  between operations  13.8 us (4%)
  blocking collectives  11.1 us (3%)
  other arithmetic  10.3 us (3%)
    all_gather x1, waiting for transfers between devices, on_device(): grad_all = lax.all_gather(grad_out, 'row', axis=0, tiled=True)  189 us
    reduce_scatter x1, waiting for transfers between devices, on_device(): lax.psum_scatter(whole * factor, 'rep', scatter_dimension=0, tiled=True)  54.4 us
    dot_general x1, matrix products, contract_rows(): lax.dot_general(left, right, (((0,), (0,)), ((), ())), preferred_element_...  17.1 us
    dot_general x1, matrix products, on_device(): lax.dot_general(block, w_out, (((1,), (1,)), ((), ())), preferred_element...  16.5 us
    all_gather x1, waiting for transfers between devices, on_device(): lax.all_gather(activation, 'col', axis=0, tiled=True)  15.1 us
    all_to_all x1, blocking collectives, summed_on_arrival(): lax.all_to_all(blocks, axis, split_axis=0, concat_axis=0, tiled=True)  11.1 us
  transfers between devices with their start and end apart: 3, of which 3 were waited for; matrix products, arithmetic and copies ran while one was open for 0% of the time, Pallas kernels for 0%

commit v1 on v0

v1 whole, which is shorter than its diff:
```python
import functools

import jax
import jax.numpy as jnp
from jax import lax
from jax.experimental import pallas as pl
from jax.experimental.pallas import tpu as pltpu
from jax.sharding import PartitionSpec as P

SQRT_TWO_PI = 0.7978845608028654
CUBIC = 0.044715
NX, NZ, NY = 4, 8, 4
NSLOT = 2 * NZ
WIDTH = 256
BF16, F32 = jnp.bfloat16, jnp.float32


def gelu_pair(values):
    inner = SQRT_TWO_PI * (values + CUBIC * values * values * values)
    bent = jnp.tanh(inner)
    output = 0.5 * values * (1.0 + bent)
    slopes = 0.5 * (1.0 + bent) + 0.5 * values * (1.0 - bent * bent) * SQRT_TWO_PI * (
        1.0 + 3.0 * CUBIC * values * values
    )
    return output, slopes


def kernel(
    factor,
    pre, w, go, outp, outw,
    G, W, PRE, ACT, SLOPE, GA, GAR, GPS, PF, SA, RA, SB, RB, SX, RX, OUTW,
    rs, gl, wl, wr, prl, prr, acr, gar, gpr, ras, rbs, rxs, ss,
):
    K = G.shape[0]
    rows = go.shape[0]
    hid = pre.shape[1]
    quarter = hid // NY
    half = rows * NZ
    width = G.shape[3]

    row, col, rep = lax.axis_index("row"), lax.axis_index("col"), lax.axis_index("rep")
    z, x = row // NX, lax.rem(row, NX)
    g, xi = x // 2, lax.rem(x, 2)
    up = {"row": lax.rem(z + 1, NZ) * NX + x}
    down = {"row": lax.rem(z + NZ - 1, NZ) * NX + x}
    side = {"row": z * NX + 2 * g + 1 - xi}
    pair = {"row": z * NX + 3 - x}
    core = {"col": 1 - col}
    y1 = rep + 1 - 2 * lax.rem(rep, 2)
    y3 = 3 - rep
    y2 = lax.rem(rep + 2, NY)
    ya, yb = (y1, y3), (y3, y1)

    def same(d):
        return lax.rem(z + NZ + d, NZ) * 2 + xi

    def other(d):
        return lax.rem(z + NZ + d, NZ) * 2 + 1 - xi

    def remote(src, dst, ssem, rsem, dev):
        pltpu.make_async_remote_copy(
            src_ref=src, dst_ref=dst, send_sem=ssem, recv_sem=rsem,
            device_id=dev, device_id_type=pl.DeviceIdType.MESH,
        ).start()

    def arrived(ref, sem):
        pltpu.make_async_copy(ref, ref, sem).wait()

    def cols(c):
        return pl.ds(pl.multiple_of(c * width, width), width)

    def group_rows(zl, group):
        return pl.ds(pl.multiple_of((zl * NX + 2 * group) * rows, 2 * rows), 2 * rows)

    mine = same(0)

    @pl.loop(0, K)
    def _(c):
        pltpu.make_async_copy(go.at[:, cols(c)], G.at[c, mine], gl.at[c]).start()

    for zl in range(NZ // 2):
        pltpu.make_async_copy(
            pre.at[group_rows(zl, g), :], PRE.at[0, pl.ds(zl * 2 * rows, 2 * rows), :], prl.at[0]
        ).start()

    @pl.loop(0, K)
    def _(c):
        pltpu.make_async_copy(w.at[:, cols(c)], W.at[c, pl.ds(0, hid), :], wl.at[c]).start()

    barrier = pltpu.get_barrier_semaphore()
    for dev in (up, down, side, pair, core, {"rep": y1}, {"rep": y3}):
        pl.semaphore_signal(barrier, inc=1, device_id=dev, device_id_type=pl.DeviceIdType.MESH)
    pl.semaphore_wait(barrier, 7)

    for zl in range(NZ // 2):
        remote(
            pre.at[group_rows(zl, 1 - g), :], PRE.at[1, pl.ds(zl * 2 * rows, 2 * rows), :],
            ss.at[4], prr.at[zl], pair,
        )

    @pl.loop(0, K)
    def _(c):
        remote(w.at[:, cols(c)], W.at[c, pl.ds(hid, hid), :], ss.at[3], wr.at[c], pair)

    def forward(c, slot, *ways):
        for way in ways:
            remote(
                G.at[c, slot], G.at[c, slot], ss.at[way], rs.at[c, slot], (up, down, side)[way]
            )

    def landed(c, slot):
        arrived(G.at[c, slot], rs.at[c, slot])

    def stage4(c):
        landed(c, same(-4))
        forward(c, same(-4), 2)

    def stage3(c):
        landed(c, same(-3))
        forward(c, same(-3), 0, 2)
        landed(c, same(3))
        forward(c, same(3), 2)

    def stage2(c):
        landed(c, same(-2))
        forward(c, same(-2), 0, 2)
        landed(c, same(2))
        forward(c, same(2), 1)
        landed(c, other(1))
        forward(c, other(1), 1)

    def stage1(c):
        landed(c, same(-1))
        forward(c, same(-1), 0)
        landed(c, same(1))
        forward(c, same(1), 1)
        landed(c, other(0))
        forward(c, other(0), 0, 1)

    def stage0(c):
        arrived(G.at[c, mine], gl.at[c])
        forward(c, mine, 0, 1, 2)

    def rest(c):
        for slot in (other(-1), other(2), other(-2), other(-3), other(3), other(-4)):
            landed(c, slot)
        arrived(W.at[c, pl.ds(0, hid), :], wl.at[c])
        arrived(W.at[c, pl.ds(hid, hid), :], wr.at[c])

    def activate(h):
        @pl.loop(0, NZ)
        def _(b):
            at = pl.ds(pl.multiple_of(b * rows, rows), rows)
            output, slopes = gelu_pair(PRE[h, at, :].astype(F32))
            SLOPE[at, pl.ds(h * hid, hid)] = slopes
            ACT[col, pl.ds(h * hid, hid), at] = output.T.astype(BF16)

    def send_act(h):
        part = ACT.at[col, pl.ds(h * hid, hid), :]
        remote(part, part, ss.at[5], acr.at[h], core)

    def wait_act():
        for h in range(2):
            part = ACT.at[1 - col, pl.ds(h * hid, hid), :]
            arrived(part, acr.at[h])

    def grad_act(c, s):
        n = NSLOT // 4
        block = G[c, pl.ds(s * n, n)].reshape(n * rows, width)
        at = pl.ds((s % 2) * n * rows, n * rows)
        GA[s // 2, at, :] += lax.dot_general(
            block, W[c], (((1,), (1,)), ((), ())), preferred_element_type=F32
        )

    def grad_w(c, p, s):
        block = G[c, pl.ds(s * NZ, NZ)].reshape(half, width)
        term = jnp.dot(ACT[s], block, preferred_element_type=F32)
        if s == 0:
            PF[p] = term
        else:
            PF[p] += term

    def part_of(p, h, q, m):
        at = pl.ds(pl.multiple_of(h * hid + q * quarter, 8), quarter)
        return PF[p, at, pl.ds(m * 128, 128)]

    def fill_a(c, p):
        for m in range(2):
            for i, q in enumerate((ya[m], y2)):
                for h in range(2):
                    SA[c, m, i, pl.ds(h * quarter, quarter), :] = part_of(p, h, q, m).astype(BF16)

    def send_a(c):
        for m in range(2):
            remote(SA.at[c, m], RA.at[c, m], ss.at[6], ras.at[c, m], {"rep": ya[m]})

    def fill_b(c, p):
        for m in range(2):
            arrived(RA.at[c, m], ras.at[c, m])
            for h in range(2):
                at = pl.ds(h * quarter, quarter)
                total = part_of(p, h, yb[m], m) + RA[c, m, 1, at, :].astype(F32)
                SB[c, m, at, :] = total.astype(BF16)

    def send_b(c):
        for m in range(2):
            remote(SB.at[c, m], RB.at[c, m], ss.at[7], rbs.at[c, m], {"rep": yb[m]})

    def fill_x(c, p):
        for m in range(2):
            arrived(RB.at[c, m], rbs.at[c, m])
            for h in range(2):
                at = pl.ds(h * quarter, quarter)
                total = (
                    part_of(p, h, rep, m)
                    + RA[c, m, 0, at, :].astype(F32)
                    + RB[c, m, at, :].astype(F32)
                )
                if h == 0:
                    OUTW[c, :, pl.ds(m * 128, 128)] = total
                else:
                    SX[c, :, pl.ds(m * 128, 128)] = total.astype(BF16)

    def send_x(c):
        remote(SX.at[c], RX.at[c], ss.at[8], rxs.at[c], pair)

    def finish(c):
        arrived(RX.at[c], rxs.at[c])
        OUTW[c] = (OUTW[c] + RX[c].astype(F32)) * factor

    def write(c):
        pltpu.make_async_copy(OUTW.at[c], outw.at[:, cols(c)], ss.at[12]).start()

    def at_tick(t, lag, body, *more):
        c = t - lag

        @pl.when((c >= 0) & (c < K))
        def _():
            body(c, *more)

    LA = 5
    DEPTH = PF.shape[0]

    def tick(t, carry):
        at_tick(t, 4, stage4)
        at_tick(t, 3, stage3)
        at_tick(t, LA, rest)
        at_tick(t, LA, grad_act, 0)
        at_tick(t, 2, stage2)
        at_tick(t, LA, grad_act, 1)
        at_tick(t, 1, stage1)
        at_tick(t, 0, stage0)
        at_tick(t, LA, grad_act, 2)
        at_tick(t, LA, grad_act, 3)

        @pl.when(t == 1)
        def _():
            GA[...] = jnp.zeros_like(GA)

        @pl.when(t == 2)
        def _():
            arrived(PRE.at[0], prl.at[0])
            activate(0)

        @pl.when(t == 3)
        def _():
            send_act(0)

        @pl.when(t == 4)
        def _():
            for zl in range(NZ // 2):
                arrived(PRE.at[1, pl.ds(zl * 2 * rows, 2 * rows), :], prr.at[zl])
            activate(1)

        @pl.when(t == 5)
        def _():
            send_act(1)
            wait_act()

        p = lax.rem(t + DEPTH - LA, DEPTH)
        at_tick(t, LA, lambda c: grad_w(c, p, 0))
        at_tick(t, LA, lambda c: grad_w(c, p, 1))
        at_tick(t, LA, lambda c: fill_a(c, p))
        at_tick(t, LA + 6, finish)
        at_tick(t, LA + 2, lambda c: fill_b(c, lax.rem(t + 2 * DEPTH - LA - 2, DEPTH)))
        at_tick(t, LA, send_a)
        at_tick(t, LA + 4, lambda c: fill_x(c, lax.rem(t + 2 * DEPTH - LA - 4, DEPTH)))
        at_tick(t, LA + 2, send_b)
        at_tick(t, LA + 6, write)
        at_tick(t, LA + 4, send_x)
        return carry

    lax.fori_loop(0, K + LA, tick, 0)

    piece = 2 * rows
    for s in range(NZ // 2):
        at = pl.ds(s * piece, piece)
        remote(GA.at[1 - col, at, :], GAR.at[at, :], ss.at[9], gar.at[s], core)

    def grad_pre(s):
        at = pl.ds(s * piece, piece)
        arrived(GAR.at[at, :], gar.at[s])
        for h in (1, 0):
            on = pl.ds(h * hid, hid)
            total = (GA[col, at, on] + GAR[at, on]) * SLOPE[at, on]
            GPS[h, at, :] = total.astype(BF16)

    def send_pre(s):
        at = pl.ds(s * piece, piece)
        here = outp.at[group_rows(s, g), :]
        remote(GPS.at[1, at, :], here, ss.at[10], gpr.at[s], pair)
        pltpu.make_async_copy(GPS.at[0, at, :], here, ss.at[11]).start()

    def slot_of(c):
        return c % DEPTH

    fill_b(K - 2, slot_of(K - 2))
    grad_pre(0)
    send_b(K - 2)
    grad_pre(1)
    send_pre(0)
    fill_b(K - 1, slot_of(K - 1))
    send_pre(1)
    send_b(K - 1)
    grad_pre(2)
    fill_x(K - 4, slot_of(K - 4))
    send_pre(2)
    grad_pre(3)
    send_x(K - 4)
    fill_x(K - 3, slot_of(K - 3))
    send_pre(3)
    send_x(K - 3)
    for c in (K - 2, K - 1):
        fill_x(c, slot_of(c))
        send_x(c)
    for c in range(K - 6, K):
        finish(c)
        write(c)

    for s in range(NZ // 2):
        arrived(outp.at[group_rows(s, 1 - g), :], gpr.at[s])
    for way in range(3):
        arrived(G.at[:, pl.ds(0, 5)], ss.at[way])
    arrived(W.at[:, pl.ds(0, hid), :], ss.at[3])
    arrived(PRE.at[1], ss.at[4])
    arrived(ACT.at[col], ss.at[5])
    arrived(SA, ss.at[6])
    arrived(SB, ss.at[7])
    arrived(SX, ss.at[8])
    arrived(GA.at[1 - col], ss.at[9])
    arrived(GPS.at[1], ss.at[10])
    arrived(GPS.at[0], ss.at[11])
    arrived(OUTW, ss.at[12])


def on_device(pre_act, w_out, grad_out):
    rows, feats = grad_out.shape
    tokens, hid = pre_act.shape
    K = feats // WIDTH
    half = rows * NZ
    quarter = hid // NY
    total_tokens = rows * lax.axis_size("row") * lax.axis_size("rep")
    factor = float(total_tokens) ** (-0.5)
    V, DMA = pltpu.VMEM, pltpu.SemaphoreType.DMA
    scratch = [
        V((K, NSLOT, rows, WIDTH), BF16),
        V((K, 2 * hid, WIDTH), BF16),
        V((2, half, hid), BF16),
        V((2, 2 * hid, half), BF16),
        V((half, 2 * hid), F32),
        V((2, half, 2 * hid), F32),
        V((half, 2 * hid), F32),
        V((2, half, hid), BF16),
        V((5, 2 * hid, WIDTH), F32),
        V((K, 2, 2, 2 * quarter, 128), BF16),
        V((K, 2, 2, 2 * quarter, 128), BF16),
        V((K, 2, 2 * quarter, 128), BF16),
        V((K, 2, 2 * quarter, 128), BF16),
        V((K, quarter, WIDTH), BF16),
        V((K, quarter, WIDTH), BF16),
        V((K, quarter, WIDTH), F32),
        DMA((K, NSLOT)), DMA((K,)), DMA((K,)), DMA((K,)), DMA((1,)), DMA((NZ // 2,)),
        DMA((2,)), DMA((NZ // 2,)), DMA((NZ // 2,)), DMA((K, 2)), DMA((K, 2)), DMA((K,)),
        DMA((13,)),
    ]
    anywhere = pl.BlockSpec(memory_space=pl.ANY)
    return pl.pallas_call(
        functools.partial(kernel, factor),
        out_shape=(
            jax.ShapeDtypeStruct((tokens, hid), BF16),
            jax.ShapeDtypeStruct((quarter, feats), F32),
        ),
        in_specs=[anywhere] * 3,
        out_specs=(anywhere, anywhere),
        scratch_shapes=scratch,
        compiler_params=pltpu.CompilerParams(
            collective_id=0, has_side_effects=True, vmem_limit_bytes=60 << 20
        ),
        name="mlp_backward",
    )(pre_act, w_out, grad_out)


def solution(mesh):
    in_specs = (P(("rep", "col"), "row"), P("row", "col"), P(("rep", "row"), "col"))
    out_specs = (P(("rep", "col"), "row"), P(("row", "rep"), "col"))
    return jax.shard_map(
        on_device, mesh=mesh, in_specs=in_specs, out_specs=out_specs, check_vma=False
    )
```

time: 328 us -> 142 us (0.43)
  waiting for transfers between devices: 259 us -> 0 us
  Pallas kernels: 0 us -> 137 us
  matrix products: 33.6 us -> 0 us
  between operations: 13.8 us -> 0.65 us
  blocking collectives: 11.1 us -> 0 us
  other arithmetic: 10.3 us -> 0 us
  local copies, waits for them, and re-layouts: 0.01 us -> 3.82 us
    all_gather x2 -> x0, waiting for transfers between devices: 204 us -> none  [the longest x1 189 us: on_device(): grad_all = lax.all_gather(grad_out, 'row', axis=0, tiled=True)]
    pallas_call x0 -> x1, Pallas kernels: none -> 137 us  [on_device(): pl.pallas_call(functools.partial(kernel, factor), out_shape=(jax.ShapeDty...]
    reduce_scatter x1 -> x0, waiting for transfers between devices: 54.4 us -> none  [on_device(): lax.psum_scatter(whole * factor, 'rep', scatter_dimension=0, tiled=True)]
    dot_general x2 -> x0, matrix products: 33.6 us -> none  [the longest x1 17.1 us: contract_rows(): lax.dot_general(left, right, (((0,), (0,)), ((), ())), preferred_element_...]
    all_to_all x1 -> x0, blocking collectives: 11.1 us -> none  [summed_on_arrival(): lax.all_to_all(blocks, axis, split_axis=0, concat_axis=0, tiled=True)]
    reduce_sum x1 -> x0, other arithmetic: 5.14 us -> none  [summed_on_arrival(): return arrived.sum(axis=0)]
    convert_element_type x1 -> x0, other arithmetic: 5.13 us -> none  [on_device(): activation = output.astype(jnp.bfloat16)]
    unnamed x2 -> x4, local copies, waits for them, and re-layouts: 0.01 us -> 3.82 us
  transfers between devices with their start and end apart: 3 -> 0, of which waited for: 3 -> 0; matrix products, arithmetic and copies ran while one was open for 0% -> 0% of each run, Pallas kernels for 0% -> 0%
where the time goes in v1:
time: 142 us
  Pallas kernels  137 us (96%)
  local copies, waits for them, and re-layouts  3.82 us (3%)
    pallas_call x1, Pallas kernels, on_device(): pl.pallas_call(functools.partial(kernel, factor), out_shape=(jax.ShapeDty...  137 us
    unnamed x4, local copies, waits for them, and re-layouts  3.82 us

profile of v1, /device:TPU:1, one launch (start us, length us, event | category | flops | bytes accessed | tf_op | source)
XLA Modules:
  0.0 141.9 jit_solution(7709011980999533296)
XLA Ops:
  0.6 137.4 %mlp_backward.1 = (bf16[2048,384]{1,0:T(8,128)(2,1)}, f32[96,3072]{1,0:T(8,128)}) custom-call(bf16[2048,384]{1,0:T(8,128)(2,1)} %pre.1, bf16[384,3072]{1,0:T(8,128)(2,1)} %w.1, bf16[128,3072]{1,0:T(8,128)(2,1)} %go.1), custom_call_target="tpu_custom_call" | custom-call | tf_op jit(solution)/shard_map/mlp_backward/pallas_call | solution.py:387
  138.1 0.0 copy-start
  138.1 2.8 %copy.7 = bf16[2048,384]{1,0:T(8,128)(2,1)} copy(bf16[2048,384]{1,0:T(8,128)(2,1)} %get-tuple-element.4) | data formatting | bytes 3145728
  140.9 0.0 copy-done
  140.9 1.0 copy.8
Async XLA Ops:
  138.1 2.8 %copy-start = (f32[96,3072]{1,0:T(8,128)S(1)}, f32[96,3072]{1,0:T(8,128)}, u32[]{:S(2)}) copy-start(f32[96,3072]{1,0:T(8,128)} %get-tuple-element.5) | copy-start | bytes 3538948

commit v2 on v0

v2 whole, which is shorter than its diff:
```python
import jax
import jax.numpy as jnp
from jax import lax
from jax.experimental import pallas as pl
from jax.experimental.pallas import tpu as pltpu
from jax.sharding import PartitionSpec as P

SQRT_TWO_PI = 0.7978845608028654
CUBIC = 0.044715
NX, NZ, NY = 4, 8, 4
NSLOT = 2 * NZ
UNIT = 128
SMALL = 0
EARLY = 4
SLOW = 10
LAGS = (0, 2, 3, 4, 5, 6)
BF16, F32 = jnp.bfloat16, jnp.float32


def gelu_pair(values):
    inner = SQRT_TWO_PI * (values + CUBIC * values * values * values)
    bent = jnp.tanh(inner)
    output = 0.5 * values * (1.0 + bent)
    slopes = 0.5 * (1.0 + bent) + 0.5 * values * (1.0 - bent * bent) * SQRT_TWO_PI * (
        1.0 + 3.0 * CUBIC * values * values
    )
    return output, slopes


def kernel(
    pre, w, go, outp, outw, outx,
    G, W, PRE, ACT, SLOPE, GA, GAR, GPS, PF, SA, RA, SB, RB, SX, OUTW,
    rs, gl, wl, wr, prl, prr, acr, gar, gpr, ras, rbs, rxs, ss,
):
    units = G.shape[0]
    K = rs.shape[0]
    BIG = K - SMALL
    rows = go.shape[0]
    hid = pre.shape[1]
    quarter = hid // NY
    half = rows * NZ

    row, col, rep = lax.axis_index("row"), lax.axis_index("col"), lax.axis_index("rep")
    z, x = row // NX, lax.rem(row, NX)
    g, xi = x // 2, lax.rem(x, 2)
    up = {"row": lax.rem(z + 1, NZ) * NX + x}
    down = {"row": lax.rem(z + NZ - 1, NZ) * NX + x}
    side = {"row": z * NX + 2 * g + 1 - xi}
    pair = {"row": z * NX + 3 - x}
    core = {"col": 1 - col}
    y1 = rep + 1 - 2 * lax.rem(rep, 2)
    y3 = 3 - rep
    y2 = lax.rem(rep + 2, NY)

    def same(d):
        return lax.rem(z + NZ + d, NZ) * 2 + xi

    def other(d):
        return lax.rem(z + NZ + d, NZ) * 2 + 1 - xi

    def remote(src, dst, ssem, rsem, dev):
        pltpu.make_async_remote_copy(
            src_ref=src, dst_ref=dst, send_sem=ssem, recv_sem=rsem,
            device_id=dev, device_id_type=pl.DeviceIdType.MESH,
        ).start()

    def arrived(ref, sem):
        pltpu.make_async_copy(ref, ref, sem).wait()

    def cols(u):
        return pl.ds(pl.multiple_of(u * UNIT, UNIT), UNIT)

    def group_rows(zl, group):
        return pl.ds(pl.multiple_of((zl * NX + 2 * group) * rows, 2 * rows), 2 * rows)

    def block_rows(b, group):
        return pl.ds(pl.multiple_of(((b // 2) * NX + 2 * group + b % 2) * rows, rows), rows)

    barrier = pltpu.get_barrier_semaphore()
    for dev in (up, down, side, pair, core, {"rep": y1}, {"rep": y3}):
        pl.semaphore_signal(barrier, inc=1, device_id=dev, device_id_type=pl.DeviceIdType.MESH)

    mine = same(0)

    @pl.loop(0, units)
    def _(u):
        pltpu.make_async_copy(go.at[:, cols(u)], G.at[u, mine], gl.at[u]).start()

    for zl in range(NZ // 2):
        pltpu.make_async_copy(
            pre.at[group_rows(zl, g), :], PRE.at[0, pl.ds(zl * 2 * rows, 2 * rows), :], prl.at[0]
        ).start()

    @pl.loop(0, units)
    def _(u):
        pltpu.make_async_copy(w.at[:, cols(u)], W.at[u, pl.ds(0, hid), :], wl.at[u]).start()

    pl.semaphore_wait(barrier, 7)

    def send_weights(u):
        remote(w.at[:, cols(u)], W.at[u, pl.ds(hid, hid), :], ss.at[3], wr.at[u], pair)

    def send_inputs():
        for u in range(4):
            send_weights(u)
        for zl in range(NZ // 2):
            remote(
                pre.at[group_rows(zl, 1 - g), :], PRE.at[1, pl.ds(zl * 2 * rows, 2 * rows), :],
                ss.at[4], prr.at[zl], pair,
            )
            send_weights(4 + 2 * zl)
            send_weights(5 + 2 * zl)

        @pl.loop(4 + NZ, units)
        def _(u):
            send_weights(u)

    class Chunk:
        def __init__(self, c, u, n):
            self.c, self.u, self.n = c, u, n

        def piece(self, slot):
            return G.at[pl.ds(self.u, self.n), slot]

        def forward(self, slot, *ways):
            for way in ways:
                ref = self.piece(slot)
                remote(ref, ref, ss.at[way], rs.at[self.c, slot], (up, down, side)[way])

        def landed(self, *slots):
            for slot in slots:
                arrived(self.piece(slot), rs.at[self.c, slot])

        def units(self):
            if self.n == 2:
                return [(self.u, 0, 0), (self.u + 1, UNIT, 1)]
            return [(self.u, 0, lax.rem(self.u, 2))]

    def big(c):
        return Chunk(c, 2 * c, 2)

    def small(c):
        return Chunk(c, c + BIG, 1)

    def pass_on(even, odd):
        def body(k):
            for parity, moves in ((0, even), (1, odd)):

                @pl.when(lax.rem(k.c, 2) == parity)
                def _():
                    for slot, *ways in moves:
                        k.landed(slot)
                        k.forward(slot, *ways)

        return body

    stage1 = pass_on(
        ((same(-1), 0, 2), (same(1), 1, 2)),
        ((same(-1), 0), (same(1), 1), (other(0), 0, 1)),
    )
    stage2 = pass_on(
        ((same(-2), 0, 2), (same(2), 1, 2)),
        ((same(-2), 0, 2), (same(2), 1), (other(1), 1)),
    )
    stage3 = pass_on(
        ((same(-3), 0), (other(2), 1), (other(-2), 0)),
        ((same(-3), 0, 2), (same(3), 2)),
    )
    stage4 = pass_on(((other(3), 1),), ((same(-4), 2),))
    kept1 = pass_on(((other(0),),), ())
    kept2 = pass_on(((other(1),), (other(-1),)), ((other(-1),),))
    kept3 = pass_on(((same(3),),), ((other(2),), (other(-2),)))
    kept4 = pass_on(((same(-4),), (other(-3),)), ((other(3),), (other(-3),)))

    def stage0(k):
        for u, _, _ in k.units():
            arrived(G.at[u, mine], gl.at[u])
        k.forward(mine, 0, 1, 2)

    def activate(h):
        @pl.loop(0, NZ)
        def _(b):
            at = pl.ds(pl.multiple_of(b * rows, rows), rows)
            output, slopes = gelu_pair(PRE[h, at, :].astype(F32))
            SLOPE[at, pl.ds(h * hid, hid)] = slopes
            ACT[col, pl.ds(h * hid, hid), at] = output.T.astype(BF16)

    def send_act(h):
        part = ACT.at[col, pl.ds(h * hid, hid), :]
        remote(part, part, ss.at[5], acr.at[h], core)

    def wait_act():
        for h in range(2):
            part = ACT.at[1 - col, pl.ds(h * hid, hid), :]
            arrived(part, acr.at[h])

    first_hop = (same(0), same(-1), same(1), other(0))
    second_hop = (same(-2), same(2), other(1), other(-1))
    third = (same(-3), same(3), other(2), other(-2))
    fourth = (same(-4), other(3), other(-3))
    fifth = (other(-4),)

    def grad_act(k, slots):
        def wide(parts):
            return parts[0] if k.n == 1 else jnp.concatenate(parts, axis=1)

        block = jnp.concatenate([wide([G[k.u + i, s] for i in range(k.n)]) for s in slots], axis=0)
        terms = lax.dot_general(
            block, wide([W[k.u + i] for i in range(k.n)]),
            (((1,), (1,)), ((), ())), preferred_element_type=F32,
        )
        for i, s in enumerate(slots):
            GA[s] += terms[i * rows : (i + 1) * rows]

    def act_first(k):
        kept1(k)
        for u, _, _ in k.units():
            arrived(W.at[u, pl.ds(0, hid), :], wl.at[u])
            arrived(W.at[u, pl.ds(hid, hid), :], wr.at[u])
        grad_act(k, first_hop)

    def act_second(k):
        kept2(k)
        grad_act(k, second_hop)

    def act_third(k):
        kept3(k)
        grad_act(k, third)

    def act_fourth(k):
        kept4(k)
        grad_act(k, fourth)

    def wide_rows(k, slot, n):
        blocks = [G[k.u + i, pl.ds(slot, n)].reshape(n * rows, UNIT) for i in range(k.n)]
        return blocks[0] if k.n == 1 else jnp.concatenate(blocks, axis=1)

    near_half = z // (NZ // 2)
    pairs = NZ // 2

    def far_pair(d):
        return lax.rem(lax.rem(z, pairs) + d, pairs)

    def act_pair(j):
        return ACT[1 - near_half, :, pl.ds(pl.multiple_of(j * 2 * rows, 2 * rows), 2 * rows)]

    def grad_w_most(k, p):
        on = pl.ds(0, k.n * UNIT)
        PF[p, :, on] = jnp.dot(
            ACT[near_half], wide_rows(k, near_half * NZ, NZ), preferred_element_type=F32
        )
        js = [far_pair(d) for d in range(1, pairs)]
        left = jnp.concatenate([act_pair(j) for j in js], axis=1)
        right = jnp.concatenate(
            [wide_rows(k, (1 - near_half) * NZ + 2 * j, 2) for j in js], axis=0
        )
        PF[p, :, on] += jnp.dot(left, right, preferred_element_type=F32)

    def grad_w_last(k, p):
        on = pl.ds(0, k.n * UNIT)
        j = far_pair(0)
        PF[p, :, on] += jnp.dot(
            act_pair(j), wide_rows(k, (1 - near_half) * NZ + 2 * j, 2), preferred_element_type=F32
        )

    def part_of(p, h, q, off):
        at = pl.ds(pl.multiple_of(h * hid + q * quarter, 8), quarter)
        return PF[p, at, pl.ds(off, UNIT)]

    def first(m):
        return y1 + m * (y3 - y1)

    def second(m):
        return y3 + m * (y1 - y3)

    def fill_a(k, p):
        for u, off, m in k.units():
            for i, q in enumerate((first(m), y2)):
                for h in range(2):
                    SA[u, i, pl.ds(h * quarter, quarter), :] = part_of(p, h, q, off).astype(BF16)

    def send_a(k):
        for u, _, m in k.units():
            remote(SA.at[u], RA.at[u], ss.at[6], ras.at[u], {"rep": first(m)})

    def fill_b(k, p):
        for u, off, m in k.units():
            arrived(RA.at[u], ras.at[u])
            for h in range(2):
                at = pl.ds(h * quarter, quarter)
                total = part_of(p, h, second(m), off) + RA[u, 1, at, :].astype(F32)
                SB[u, at, :] = total.astype(BF16)

    def send_b(k):
        for u, _, m in k.units():
            remote(SB.at[u], RB.at[u], ss.at[7], rbs.at[u], {"rep": second(m)})

    def fill_x(k, p):
        for u, off, m in k.units():
            arrived(RB.at[u], rbs.at[u])
            for h in range(2):
                at = pl.ds(h * quarter, quarter)
                total = (
                    part_of(p, h, rep, off)
                    + RA[u, 0, at, :].astype(F32)
                    + RB[u, at, :].astype(F32)
                )
                if h == 0:
                    OUTW[u] = total
                else:
                    SX[u] = total.astype(BF16)

    def send_x(k):
        for u, _, _ in k.units():
            remote(SX.at[u], outx.at[:, cols(u)], ss.at[8], rxs.at[u], pair)
            pltpu.make_async_copy(OUTW.at[u], outw.at[:, cols(u)], ss.at[12]).start()

    def send_sums(slots):
        for s in slots:
            b = s - NZ * (1 - col)

            @pl.when((b >= 0) & (b < NZ))
            def _():
                remote(GA.at[s], GAR.at[b], ss.at[9], gar.at[b], core)

    def on_mine(slots, body):
        for s in slots:
            b = s - NZ * col

            @pl.when((b >= 0) & (b < NZ))
            def _():
                body(s, b)

    def grad_pre(s, b):
        at = pl.ds(pl.multiple_of(b * rows, rows), rows)
        arrived(GAR.at[b], gar.at[b])
        for h in (1, 0):
            on = pl.ds(h * hid, hid)
            total = (GA[s, :, on] + GAR[b, :, on]) * SLOPE[at, on]
            GPS[h, b] = total.astype(BF16)

    def send_pre(s, b):
        here = outp.at[block_rows(b, g), :]
        remote(GPS.at[1, b], here, ss.at[10], gpr.at[b], pair)
        pltpu.make_async_copy(GPS.at[0, b], here, ss.at[11]).start()

    def at_tick(t, lag, body, *more, lo=0, hi=None):
        c = t - lag
        hi = K if hi is None else hi

        @pl.when((c >= lo) & (c < min(hi, BIG)))
        def _():
            body(big(c), *more)

        if hi > BIG:

            @pl.when((c >= BIG) & (c < hi))
            def _():
                body(small(c), *more)

    DEPTH = PF.shape[0]
    L0, L1, L2, L3, L4, LA = LAGS
    groups = ((first_hop, L1), (second_hop, L2), (third, L3), (fourth, L4))

    def tick(t, carry):
        def slot_at(lag):
            return lax.rem(t + 2 * DEPTH - lag, DEPTH)

        def chain(lag, body, slots, lo=0, hi=None):
            more = (slot_at(lag),) if slots else ()
            at_tick(t, lag, body, *more, lo=lo, hi=hi)

        at_tick(t, L0, stage0)
        at_tick(t, L4, stage4)
        at_tick(t, L3, stage3)
        at_tick(t, L4, act_fourth)
        at_tick(t, L2, stage2)
        at_tick(t, L3, act_first, hi=SLOW)
        at_tick(t, L3, act_second, hi=SLOW)
        at_tick(t, L3, act_third)
        at_tick(t, L1, stage1)
        at_tick(t, L2, act_second, lo=SLOW)
        at_tick(t, L1, act_first, lo=SLOW)

        @pl.when(t == 0)
        def _():
            send_inputs()

        @pl.when(t == 1)
        def _():
            GA[...] = jnp.zeros_like(GA)

        @pl.when(t == 3)
        def _():
            arrived(PRE.at[0], prl.at[0])
            activate(0)

        @pl.when(t == 4)
        def _():
            send_act(0)

        @pl.when(t == 8)
        def _():
            for zl in range(NZ // 2):
                arrived(PRE.at[1, pl.ds(zl * 2 * rows, 2 * rows), :], prr.at[zl])
            activate(1)

        @pl.when(t == 9)
        def _():
            send_act(1)
            wait_act()

        for slots, lag in groups:

            @pl.when(t == K - 1 + lag)
            def _():
                send_sums(slots)

        def tail(k):
            k.landed(other(-4))

        at_tick(t, LA, tail)
        chain(LA + 3, grad_w_most, True, 0, EARLY)
        for lag, lo, hi in ((LA + 3, 0, EARLY), (LA, EARLY, None)):
            chain(lag, grad_w_last, True, lo, hi)
            chain(lag, fill_a, True, lo, hi)
        at_tick(t, LA, grad_act, fifth)
        for lag, lo, hi in ((LA + 3, 0, EARLY), (LA, EARLY, None)):
            chain(lag, send_a, False, lo, hi)
        chain(L4, grad_w_most, True, EARLY)

        @pl.when(t == K + LA - 1)
        def _():
            send_sums(fifth)

        for slots, lag in groups:

            @pl.when(t == K + lag)
            def _():
                on_mine(slots, grad_pre)

        for lag, lo, hi in ((LA + 3, 0, EARLY), (LA, EARLY, None)):
            chain(lag + 1, fill_b, True, lo, hi)
            chain(lag + 2, fill_x, True, lo, hi)
            chain(lag + 1, send_b, False, lo, hi)
            chain(lag + 2, send_x, False, lo, hi)

        for slots, lag in groups:

            @pl.when(t == K + lag)
            def _():
                on_mine(slots, send_pre)

        return carry

    lax.fori_loop(0, K + LA, tick, 0)

    def last(c):
        return big(c) if c < BIG else small(c)

    on_mine(fifth, grad_pre)
    fill_x(last(K - 2), (K - 2) % DEPTH)
    fill_b(last(K - 1), (K - 1) % DEPTH)
    on_mine(fifth, send_pre)
    send_x(last(K - 2))
    send_b(last(K - 1))
    fill_x(last(K - 1), (K - 1) % DEPTH)
    send_x(last(K - 1))
    @pl.loop(0, units)
    def _(u):
        arrived(outx.at[:, cols(u)], rxs.at[u])

    for b in range(NZ):
        arrived(outp.at[block_rows(b, 1 - g), :], gpr.at[b])
    for way in range(3):
        arrived(G.at[:, pl.ds(0, 5)], ss.at[way])
    arrived(W.at[:, pl.ds(0, hid), :], ss.at[3])
    arrived(PRE.at[1], ss.at[4])
    arrived(ACT.at[col], ss.at[5])
    arrived(SA, ss.at[6])
    arrived(SB, ss.at[7])
    arrived(SX, ss.at[8])
    arrived(GA.at[pl.ds(0, NZ)], ss.at[9])
    arrived(GPS.at[1], ss.at[10])
    arrived(GPS.at[0], ss.at[11])
    arrived(OUTW, ss.at[12])


def on_device(pre_act, w_out, grad_out):
    rows, feats = grad_out.shape
    tokens, hid = pre_act.shape
    units = feats // UNIT
    K = (units - SMALL) // 2 + SMALL
    half = rows * NZ
    quarter = hid // NY
    total_tokens = rows * lax.axis_size("row") * lax.axis_size("rep")
    factor = float(total_tokens) ** (-0.5)
    V, DMA = pltpu.VMEM, pltpu.SemaphoreType.DMA
    scratch = [
        V((units, NSLOT, rows, UNIT), BF16),
        V((units, 2 * hid, UNIT), BF16),
        V((2, half, hid), BF16),
        V((2, 2 * hid, half), BF16),
        V((half, 2 * hid), F32),
        V((NSLOT, rows, 2 * hid), F32),
        V((NZ, rows, 2 * hid), F32),
        V((2, NZ, rows, hid), BF16),
        V((8, 2 * hid, 2 * UNIT), F32),
        V((units, 2, 2 * quarter, UNIT), BF16),
        V((units, 2, 2 * quarter, UNIT), BF16),
        V((units, 2 * quarter, UNIT), BF16),
        V((units, 2 * quarter, UNIT), BF16),
        V((units, quarter, UNIT), BF16),
        V((units, quarter, UNIT), F32),
        DMA((K, NSLOT)), DMA((units,)), DMA((units,)), DMA((units,)), DMA((1,)),
        DMA((NZ // 2,)), DMA((2,)), DMA((NZ,)), DMA((NZ,)), DMA((units,)), DMA((units,)),
        DMA((units,)), DMA((13,)),
    ]
    anywhere = pl.BlockSpec(memory_space=pl.ANY)
    grad_pre, kept, came = pl.pallas_call(
        kernel,
        out_shape=(
            jax.ShapeDtypeStruct((tokens, hid), BF16),
            jax.ShapeDtypeStruct((quarter, feats), F32),
            jax.ShapeDtypeStruct((quarter, feats), BF16),
        ),
        in_specs=[anywhere] * 3,
        out_specs=(anywhere,) * 3,
        scratch_shapes=scratch,
        compiler_params=pltpu.CompilerParams(
            collective_id=0, has_side_effects=True, vmem_limit_bytes=60 << 20
        ),
        name="mlp_backward",
    )(pre_act, w_out, grad_out)
    return grad_pre, (kept + came.astype(F32)) * factor


def solution(mesh):
    in_specs = (P(("rep", "col"), "row"), P("row", "col"), P(("rep", "row"), "col"))
    out_specs = (P(("rep", "col"), "row"), P(("row", "rep"), "col"))
    return jax.shard_map(
        on_device, mesh=mesh, in_specs=in_specs, out_specs=out_specs, check_vma=False
    )
```

time: 328 us -> 132 us (0.40)
  waiting for transfers between devices: 259 us -> 0 us
  Pallas kernels: 0 us -> 127 us
  matrix products: 33.6 us -> 0 us
  between operations: 13.8 us -> 0.65 us
  blocking collectives: 11.1 us -> 0 us
  other arithmetic: 10.3 us -> 2.7 us
    all_gather x2 -> x0, waiting for transfers between devices: 204 us -> none  [the longest x1 189 us: on_device(): grad_all = lax.all_gather(grad_out, 'row', axis=0, tiled=True)]
    pallas_call x0 -> x1, Pallas kernels: none -> 127 us  [on_device(): pl.pallas_call(kernel, out_shape=(jax.ShapeDtypeStruct((tokens, hid), BF1...]
    reduce_scatter x1 -> x0, waiting for transfers between devices: 54.4 us -> none  [on_device(): lax.psum_scatter(whole * factor, 'rep', scatter_dimension=0, tiled=True)]
    dot_general x2 -> x0, matrix products: 33.6 us -> none  [the longest x1 17.1 us: contract_rows(): lax.dot_general(left, right, (((0,), (0,)), ((), ())), preferred_element_...]
    all_to_all x1 -> x0, blocking collectives: 11.1 us -> none  [summed_on_arrival(): lax.all_to_all(blocks, axis, split_axis=0, concat_axis=0, tiled=True)]
    reduce_sum x1 -> x0, other arithmetic: 5.14 us -> none  [summed_on_arrival(): return arrived.sum(axis=0)]
    convert_element_type x1 -> x0, other arithmetic: 5.13 us -> none  [on_device(): activation = output.astype(jnp.bfloat16)]
  transfers between devices with their start and end apart: 3 -> 0, of which waited for: 3 -> 0; matrix products, arithmetic and copies ran while one was open for 0% -> 0% of each run, Pallas kernels for 0% -> 0%
where the time goes in v2:
time: 132 us
  Pallas kernels  127 us (96%)
  other arithmetic  2.7 us (2%)
    pallas_call x1, Pallas kernels, on_device(): pl.pallas_call(kernel, out_shape=(jax.ShapeDtypeStruct((tokens, hid), BF1...  127 us
    mul x1, other arithmetic, on_device(): return (grad_pre, (kept + came.astype(F32)) * factor)  2.7 us

profile of v2, /device:TPU:1, one launch (start us, length us, event | category | flops | bytes accessed | tf_op | source)
XLA Modules:
  0.0 132.0 jit_solution(15875873693051714058)
XLA Ops:
  0.6 127.5 %mlp_backward.1 = (bf16[2048,384]{1,0:T(8,128)(2,1)}, f32[96,3072]{1,0:T(8,128)}, bf16[96,3072]{1,0:T(8,128)(2,1)}) custom-call(bf16[2048,384]{1,0:T(8,128)(2,1)} %pre.1, bf16[384,3072]{1,0:T(8,128)(2,1)} %w.1, bf16[128,3072]{1,0:T(8,128)(2,1)} %go.1), custom_call_target="tpu_custom_call" | custom-call | tf_op jit(solution)/shard_map/mlp_backward/pallas_call | solution.py:520
  128.1 0.0 copy-start
  128.1 2.7 %add_multiply_fusion = f32[96,3072]{1,0:T(8,128)} fusion(f32[96,3072]{1,0:T(8,128)} %get-tuple-element.6, bf16[96,3072]{1,0:T(8,128)(2,1)} %get-tuple-element.7), kind=kLoop, calls=%fused_computation | loop fusion | flops 884736 | bytes 2949120 | tf_op jit(solution)/shard_map/mul | solution.py:535
  130.8 0.0 copy-done
  130.8 1.1 copy.6
Async XLA Ops:
  128.1 2.7 %copy-start = (bf16[2048,384]{1,0:T(8,128)(2,1)S(1)}, bf16[2048,384]{1,0:T(8,128)(2,1)}, u32[]{:S(2)}) copy-start(bf16[2048,384]{1,0:T(8,128)(2,1)} %get-tuple-element.10) | copy-start | bytes 4718596

commit v3 on v2

--- a/solution.py
+++ b/solution.py
@@ -11,8 +11,8 @@
 NSLOT = 2 * NZ
 UNIT = 128
 SMALL = 0
-EARLY = 4
-SLOW = 10
+EARLY = 2
+MID, SLOW = 8, 10
 LAGS = (0, 2, 3, 4, 5, 6)
 BF16, F32 = jnp.bfloat16, jnp.float32
 
@@ -100,18 +100,20 @@
     def send_weights(u):
         remote(w.at[:, cols(u)], W.at[u, pl.ds(hid, hid), :], ss.at[3], wr.at[u], pair)
 
+    def send_act_inputs(zl):
+        remote(
+            pre.at[group_rows(zl, 1 - g), :], PRE.at[1, pl.ds(zl * 2 * rows, 2 * rows), :],
+            ss.at[4], prr.at[zl], pair,
+        )
+
     def send_inputs():
-        for u in range(4):
-            send_weights(u)
         for zl in range(NZ // 2):
-            remote(
-                pre.at[group_rows(zl, 1 - g), :], PRE.at[1, pl.ds(zl * 2 * rows, 2 * rows), :],
-                ss.at[4], prr.at[zl], pair,
-            )
-            send_weights(4 + 2 * zl)
-            send_weights(5 + 2 * zl)
-
-        @pl.loop(4 + NZ, units)
+            if zl % 2 == 0:
+                send_weights(zl)
+                send_weights(zl + 1)
+            send_act_inputs(zl)
+
+        @pl.loop(NZ // 2, units)
         def _(u):
             send_weights(u)
 
@@ -223,6 +225,14 @@
         kept2(k)
         grad_act(k, second_hop)
 
+    def act_near(k):
+        kept1(k)
+        kept2(k)
+        for u, _, _ in k.units():
+            arrived(W.at[u, pl.ds(0, hid), :], wl.at[u])
+            arrived(W.at[u, pl.ds(hid, hid), :], wr.at[u])
+        grad_act(k, first_hop + second_hop)
+
     def act_third(k):
         kept3(k)
         grad_act(k, third)
@@ -373,12 +383,13 @@
         at_tick(t, L0, stage0)
         at_tick(t, L4, stage4)
         at_tick(t, L3, stage3)
+        at_tick(t, L2, stage2)
+        at_tick(t, L1, stage1)
+        at_tick(t, L4, act_near, hi=MID)
+        at_tick(t, L4, act_third, hi=MID)
+        at_tick(t, L3, act_near, lo=MID, hi=SLOW)
         at_tick(t, L4, act_fourth)
-        at_tick(t, L2, stage2)
-        at_tick(t, L3, act_first, hi=SLOW)
-        at_tick(t, L3, act_second, hi=SLOW)
-        at_tick(t, L3, act_third)
-        at_tick(t, L1, stage1)
+        at_tick(t, L3, act_third, lo=MID)
         at_tick(t, L2, act_second, lo=SLOW)
         at_tick(t, L1, act_first, lo=SLOW)
 
@@ -399,13 +410,13 @@
         def _():
             send_act(0)
 
-        @pl.when(t == 8)
+        @pl.when(t == 6)
         def _():
             for zl in range(NZ // 2):
                 arrived(PRE.at[1, pl.ds(zl * 2 * rows, 2 * rows), :], prr.at[zl])
             activate(1)
 
-        @pl.when(t == 9)
+        @pl.when(t == 7)
         def _():
             send_act(1)
             wait_act()
@@ -420,12 +431,12 @@
             k.landed(other(-4))
 
         at_tick(t, LA, tail)
-        chain(LA + 3, grad_w_most, True, 0, EARLY)
-        for lag, lo, hi in ((LA + 3, 0, EARLY), (LA, EARLY, None)):
+        chain(LA + 1, grad_w_most, True, 0, EARLY)
+        for lag, lo, hi in ((LA + 1, 0, EARLY), (LA, EARLY, None)):
             chain(lag, grad_w_last, True, lo, hi)
             chain(lag, fill_a, True, lo, hi)
         at_tick(t, LA, grad_act, fifth)
-        for lag, lo, hi in ((LA + 3, 0, EARLY), (LA, EARLY, None)):
+        for lag, lo, hi in ((LA + 1, 0, EARLY), (LA, EARLY, None)):
             chain(lag, send_a, False, lo, hi)
         chain(L4, grad_w_most, True, EARLY)
 
@@ -439,7 +450,7 @@
             def _():
                 on_mine(slots, grad_pre)
 
-        for lag, lo, hi in ((LA + 3, 0, EARLY), (LA, EARLY, None)):
+        for lag, lo, hi in ((LA + 1, 0, EARLY), (LA, EARLY, None)):
             chain(lag + 1, fill_b, True, lo, hi)
             chain(lag + 2, fill_x, True, lo, hi)
             chain(lag + 1, send_b, False, lo, hi)

time: 132 us -> 130 us (0.985)
  Pallas kernels: 127 us -> 125 us
    pallas_call x1, Pallas kernels: 127 us -> 125 us  [on_device(): pl.pallas_call(kernel, out_shape=(jax.ShapeDtypeStruct((tokens, hid), BF1...]
where the time goes in v3:
time: 130 us
  Pallas kernels  125 us (96%)
  other arithmetic  2.7 us (2%)
    pallas_call x1, Pallas kernels, on_device(): pl.pallas_call(kernel, out_shape=(jax.ShapeDtypeStruct((tokens, hid), BF1...  125 us
    mul x1, other arithmetic, on_device(): return (grad_pre, (kept + came.astype(F32)) * factor)  2.7 us

profile of v3, /device:TPU:1, one launch (start us, length us, event | category | flops | bytes accessed | tf_op | source)
XLA Modules:
  0.0 129.7 jit_solution(3604633807748033432)
XLA Ops:
  0.6 125.2 %mlp_backward.1 = (bf16[2048,384]{1,0:T(8,128)(2,1)}, f32[96,3072]{1,0:T(8,128)}, bf16[96,3072]{1,0:T(8,128)(2,1)}) custom-call(bf16[2048,384]{1,0:T(8,128)(2,1)} %pre.1, bf16[384,3072]{1,0:T(8,128)(2,1)} %w.1, bf16[128,3072]{1,0:T(8,128)(2,1)} %go.1), custom_call_target="tpu_custom_call" | custom-call | tf_op jit(solution)/shard_map/mlp_backward/pallas_call | solution.py:531
  125.8 0.0 copy-start
  125.8 2.7 %add_multiply_fusion = f32[96,3072]{1,0:T(8,128)} fusion(f32[96,3072]{1,0:T(8,128)} %get-tuple-element.6, bf16[96,3072]{1,0:T(8,128)(2,1)} %get-tuple-element.7), kind=kLoop, calls=%fused_computation | loop fusion | flops 884736 | bytes 2949120 | tf_op jit(solution)/shard_map/mul | solution.py:546
  128.5 0.0 copy-done
  128.6 1.1 copy.6
Async XLA Ops:
  125.8 2.7 %copy-start = (bf16[2048,384]{1,0:T(8,128)(2,1)S(1)}, bf16[2048,384]{1,0:T(8,128)(2,1)}, u32[]{:S(2)}) copy-start(bf16[2048,384]{1,0:T(8,128)(2,1)} %get-tuple-element.10) | copy-start | bytes 4718596

commit v4 on v3

--- a/solution.py
+++ b/solution.py
@@ -290,12 +290,13 @@
                     SA[u, i, pl.ds(h * quarter, quarter), :] = part_of(p, h, q, off).astype(BF16)
 
     def send_a(k):
-        for u, _, m in k.units():
-            remote(SA.at[u], RA.at[u], ss.at[6], ras.at[u], {"rep": first(m)})
+        for i in (1, 0):
+            for u, _, m in k.units():
+                remote(SA.at[u, i], RA.at[u, i], ss.at[6], ras.at[u, i], {"rep": first(m)})
 
     def fill_b(k, p):
         for u, off, m in k.units():
-            arrived(RA.at[u], ras.at[u])
+            arrived(RA.at[u, 1], ras.at[u, 1])
             for h in range(2):
                 at = pl.ds(h * quarter, quarter)
                 total = part_of(p, h, second(m), off) + RA[u, 1, at, :].astype(F32)
@@ -307,6 +308,7 @@
 
     def fill_x(k, p):
         for u, off, m in k.units():
+            arrived(RA.at[u, 0], ras.at[u, 0])
             arrived(RB.at[u], rbs.at[u])
             for h in range(2):
                 at = pl.ds(h * quarter, quarter)
@@ -524,7 +526,7 @@
         V((units, quarter, UNIT), BF16),
         V((units, quarter, UNIT), F32),
         DMA((K, NSLOT)), DMA((units,)), DMA((units,)), DMA((units,)), DMA((1,)),
-        DMA((NZ // 2,)), DMA((2,)), DMA((NZ,)), DMA((NZ,)), DMA((units,)), DMA((units,)),
+        DMA((NZ // 2,)), DMA((2,)), DMA((NZ,)), DMA((NZ,)), DMA((units, 2)), DMA((units,)),
         DMA((units,)), DMA((13,)),
     ]
     anywhere = pl.BlockSpec(memory_space=pl.ANY)

time: 130 us -> 130 us (level)
  no operation moved by 1% of the time
where the time goes in v4:
time: 130 us
  Pallas kernels  126 us (97%)
  other arithmetic  2.7 us (2%)
    pallas_call x1, Pallas kernels, on_device(): pl.pallas_call(kernel, out_shape=(jax.ShapeDtypeStruct((tokens, hid), BF1...  126 us
    mul x1, other arithmetic, on_device(): return (grad_pre, (kept + came.astype(F32)) * factor)  2.7 us

profile of v4, /device:TPU:1, one launch (start us, length us, event | category | flops | bytes accessed | tf_op | source)
XLA Modules:
  0.0 130.0 jit_solution(15131672024973385613)
XLA Ops:
  0.6 125.5 %mlp_backward.1 = (bf16[2048,384]{1,0:T(8,128)(2,1)}, f32[96,3072]{1,0:T(8,128)}, bf16[96,3072]{1,0:T(8,128)(2,1)}) custom-call(bf16[2048,384]{1,0:T(8,128)(2,1)} %pre.1, bf16[384,3072]{1,0:T(8,128)(2,1)} %w.1, bf16[128,3072]{1,0:T(8,128)(2,1)} %go.1), custom_call_target="tpu_custom_call" | custom-call | tf_op jit(solution)/shard_map/mlp_backward/pallas_call | solution.py:533
  126.1 0.0 copy-start
  126.2 2.7 %add_multiply_fusion = f32[96,3072]{1,0:T(8,128)} fusion(f32[96,3072]{1,0:T(8,128)} %get-tuple-element.6, bf16[96,3072]{1,0:T(8,128)(2,1)} %get-tuple-element.7), kind=kLoop, calls=%fused_computation | loop fusion | flops 884736 | bytes 2949120 | tf_op jit(solution)/shard_map/mul | solution.py:548
  128.9 0.0 copy-done
  128.9 1.1 copy.6
Async XLA Ops:
  126.1 2.7 %copy-start = (bf16[2048,384]{1,0:T(8,128)(2,1)S(1)}, bf16[2048,384]{1,0:T(8,128)(2,1)}, u32[]{:S(2)}) copy-start(bf16[2048,384]{1,0:T(8,128)(2,1)} %get-tuple-element.10) | copy-start | bytes 4718596
